TPU v7x, 128 devices: a whole 4x4x4 slice. The times are simulated.
128 devices in a mesh: grp: 4 (over z), slab: 32 (over x, y, core).
Axes of the slice: x: 4, y: 4, z: 4, core: 2. Of those that a mesh axis runs over, the one named last changes fastest.
Arguments:
- probes: float32 [64, 512, 8, 512], P(None, 'slab', None, 'grp'), may hold values from -6 to 6
- courant: float32 [512, 8, 512], P('slab', None, 'grp'), may hold values from 0.02 to 0.18
- rec_cell: int32 [8192], P(('grp', 'slab')), may hold values from 0 to 16383
- rec_owner: int32 [8192, 1], P(('grp', 'slab')), may hold values from 0 to 31; in each aligned block of 64 rows (0 to 63, 64 to 127, ...) at most 8 rows name the same one
- trace_weight: float32 [8192], P(('grp', 'slab')), may hold values from 1 to 10
Outputs:
- wavefield: float32 [64, 512, 8, 512], P(None, 'slab', None, 'grp')
- q_basis: float32 [32768, 256], P(('grp', 'slab'))
- r_factor: float32 [64, 64], replicated
Inputs may be any that keep to these rules, and one draw needn't show every extreme that they name: `rec_owner`: among the receivers of one device no owner is named by more than 8; in every draw some device names some owner exactly 8 times.
All inputs are finite; a program needn't handle non-finite values.
Results may differ from a plain program's by a relative error of at most 0.00016.
Values sent between devices are 32-bit elements; how exact they have to be, the bound alone decides.
A program may use at most 192 MiB of HBM per device.

v0:
```python
import math
import jax
import jax.numpy as jnp
from jax import lax
from jax.sharding import PartitionSpec as P

PROBES = 64
CX = 16
CY = 8
CZ = 128
STEPS = 4
stencil_weights = (-205.0 / 72.0, 8.0 / 5.0, -1.0 / 5.0, 8.0 / 315.0, -1.0 / 560.0)


def with_halo(block, sides, width):
    for axis, dim in sides:
        count = lax.axis_size(axis)
        forward = [(i, i + 1) for i in range(count - 1)]
        backward = [(target, source) for source, target in forward]
        low = lax.ppermute(
            lax.slice_in_dim(block, block.shape[dim] - width, None, axis=dim), axis, forward
        )
        high = lax.ppermute(lax.slice_in_dim(block, 0, width, axis=dim), axis, backward)
        block = jnp.concatenate([low, block, high], axis=dim)
    return block


def laplace(padded):
    size_x = padded.shape[1] - 8
    size_y = padded.shape[2] - 8
    size_z = padded.shape[3] - 8
    center = padded[:, 4 : 4 + size_x, 4 : 4 + size_y, 4 : 4 + size_z]
    total = 3.0 * stencil_weights[0] * center
    for offset in range(1, 5):
        beside_all = padded[:, 4 + offset : 4 + offset + size_x, 4 : 4 + size_y, 4 : 4 + size_z]
        beside_all = (
            beside_all + padded[:, 4 - offset : 4 - offset + size_x, 4 : 4 + size_y, 4 : 4 + size_z]
        )
        beside_all = (
            beside_all + padded[:, 4 : 4 + size_x, 4 + offset : 4 + offset + size_y, 4 : 4 + size_z]
        )
        beside_all = (
            beside_all + padded[:, 4 : 4 + size_x, 4 - offset : 4 - offset + size_y, 4 : 4 + size_z]
        )
        beside_all = (
            beside_all + padded[:, 4 : 4 + size_x, 4 : 4 + size_y, 4 + offset : 4 + offset + size_z]
        )
        beside_all = (
            beside_all + padded[:, 4 : 4 + size_x, 4 : 4 + size_y, 4 - offset : 4 - offset + size_z]
        )
        total = total + stencil_weights[offset] * beside_all
    return total


def pad_middle(field):
    return jnp.pad(field, ((0, 0), (0, 0), (4, 4), (0, 0)))


def per_device(probes, courant, rec_cell, rec_owner, trace_weight):
    n_slab = lax.axis_size("slab")
    n_group = lax.axis_size("grp")
    rec_count = rec_cell.shape[0]
    capacity = max(2, 4 * rec_count // n_slab)
    cells = CX * CY * CZ
    picker = (jnp.arange(cells, dtype=jnp.int32)[:, None] == rec_cell[None, :]).astype(jnp.float32)
    speed = courant[None]
    previous = probes
    current = probes
    samples = []
    for moment in range(STEPS):
        extended = with_halo(current, (("grp", 3), ("slab", 1)), 4)
        advanced = 2.0 * current - previous + speed * laplace(pad_middle(extended))
        previous = current
        current = advanced
        samples.append(
            jnp.dot(
                current.reshape(PROBES, cells),
                picker,
                preferred_element_type=jnp.float32,
                precision=lax.Precision.HIGHEST,
            )
        )
    traces = jnp.stack(samples)
    rows = jnp.transpose(traces, (2, 0, 1)) * trace_weight[:, None, None]
    rows = rows.reshape(rec_count, STEPS * PROBES)
    sketch = rows.reshape(rec_count * STEPS, PROBES)
    gram = jnp.dot(
        sketch.T, sketch, preferred_element_type=jnp.float32, precision=lax.Precision.HIGHEST
    )
    owners = rec_owner[:, 0]
    hits = (owners[:, None] == jnp.arange(n_slab, dtype=jnp.int32)[None, :]).astype(jnp.int32)
    before = jnp.cumsum(hits, axis=0) - hits
    slots = jnp.sum(before * hits, axis=1)
    target = owners * capacity + slots
    placer = (target[:, None] == jnp.arange(n_slab * capacity, dtype=jnp.int32)[None, :]).astype(
        jnp.float32
    )
    outgoing = jnp.dot(
        placer.T, rows, preferred_element_type=jnp.float32, precision=lax.Precision.HIGHEST
    )
    incoming = lax.all_to_all(
        outgoing.reshape(n_slab, capacity, STEPS * PROBES),
        "slab",
        split_axis=0,
        concat_axis=0,
        tiled=True,
    )
    incoming = incoming.reshape(n_slab * capacity, STEPS * PROBES)
    lower = jnp.linalg.cholesky(lax.psum(gram, ("grp", "slab")))
    row_count = rec_count * n_slab * n_group * STEPS
    r_factor = lower.T / math.sqrt(row_count)
    solved = jax.scipy.linalg.solve_triangular(
        lower, incoming.reshape(n_slab * capacity * STEPS, PROBES).T, lower=True
    )
    q_basis = (solved.T * math.sqrt(row_count)).reshape(n_slab * capacity, STEPS * PROBES)
    return (current, q_basis, r_factor)


def solution(mesh):
    return jax.shard_map(
        per_device,
        mesh=mesh,
        in_specs=(
            P(None, "slab", None, "grp"),
            P("slab", None, "grp"),
            P(("grp", "slab")),
            P(("grp", "slab"), None),
            P(("grp", "slab")),
        ),
        out_specs=(P(None, "slab", None, "grp"), P(("grp", "slab"), None), P()),
        check_vma=False,
    )
```

profile of v0, /device:TPU:1, one launch (start us, length us, event | category | flops | bytes accessed | tf_op | source)
XLA Modules:
  0.0 824.6 jit_solution(537160318076101467)
XLA Ops:
  0.6 8.2 fusion.137
  8.8 3.7 copy.123
  13.8 3.7 copy.122
  17.5 5.0 collective-permute-start
  22.9 4.6 copy.90
  27.5 4.5 copy.89
  32.0 4.7 pad_maximum_fusion.21
  36.7 4.8 collective-permute-start.3
  41.5 2.1 collective-permute-start.2
  43.6 20.9 %collective-permute-done.3 = f32[64,4,8,136]{3,2,1,0:T(8,128)S(1)} collective-permute-done((f32[64,4,8,136]{3,2,1,0:T(8,128)S(1)}, f32[64,4,8,136]{3,2,1,0:T(8,128)S(1)}, u32[]{:S(2)}, u32[]{:S(2)}) %collective-permute-start.3) | collective-permute-done | bytes 1114144 | tf_op jit(solution)/shard_map/ppermute | solution.py:20
  64.5 4.4 collective-permute-done.2
  68.9 11.0 %pad_maximum_fusion = (f32[64,20,8,136]{3,2,1,0:T(8,128)}, f32[64,20,8,136]{3,2,1,0:T(8,128)}) fusion(f32[64,4,8,136]{3,2,1,0:T(8,128)S(1)} %collective-permute-done.2, f32[64,16,8,4]{3,2,1,0:T(8,128)S(1)} %copy-done.8, f32[64,16,8,128]{3,2,1,0:T(8,128)S(1)} %copy-done.5, f32[64,16,8,4]{3,2,1,0:T(8,128)S(1)} %copy-done.11, ...), kind=kLoop, calls=%fused_computation.67 | loop fusion | flops 8355840 | bytes 17825792 | tf_op jit(solution)/shard_map/concatenate | solution.py:24
  79.9 12.4 %select_maximum_fusion.12 = f32[64,24,16,136]{3,2,1,0:T(8,128)} fusion(f32[64,4,8,136]{3,2,1,0:T(8,128)S(1)} %collective-permute-done.2, f32[64,4,8,136]{3,2,1,0:T(8,128)S(1)} %collective-permute-done.3, f32[64,16,8,4]{3,2,1,0:T(8,128)S(1)} %copy-done.8, f32[64,16,8,128]{3,2,1,0:T(8,128)S(1)} %copy-done.5, f32[64,16,8,4]{3,2,1,0:T(8,128)S(1)} %copy-done.11), kind=kLoop, calls=%fused_computation.14 | loop fusion | flops 40108032 | bytes 20054016 | tf_op jit(solution)/shard_map/concatenate | solution.py:24
  92.3 88.4 %fusion.1 = f32[64,16,8,128]{3,2,1,0:T(8,128)} fusion(f32[64,16,8,128]{3,2,1,0:T(8,128)} %param.5, f32[64,16,8,4]{3,2,1,0:T(8,128)} %copy.89, f32[64,16,8,4]{3,2,1,0:T(8,128)} %copy.90, f32[64,24,16,136]{3,2,1,0:T(8,128)} %select_maximum_fusion.12, f32[64,20,8,136]{3,2,1,0:T(8,128)} %get-tuple-element.34, f32[64,20,8,136]{3,2,1,0:T(8,128)} %get-tuple-element.33, ...), kind=kLoop, calls=%fused_computation.76 | loop fusion | flops 42991616 | bytes 75825152 | tf_op jit(solution)/shard_map/add | solution.py:72
  180.7 8.2 fusion.136
  188.9 3.7 copy.94
  193.9 3.7 copy.93
  197.6 4.7 collective-permute-start.4
  202.4 4.6 copy.96
  207.0 4.5 copy.95
  211.5 4.7 pad_maximum_fusion.18
  216.1 3.4 collective-permute-start.7
  219.6 2.3 collective-permute-start.6
  221.9 20.6 %collective-permute-done.7 = f32[64,4,8,136]{3,2,1,0:T(8,128)S(1)} collective-permute-done((f32[64,4,8,136]{3,2,1,0:T(8,128)S(1)}, f32[64,4,8,136]{3,2,1,0:T(8,128)S(1)}, u32[]{:S(2)}, u32[]{:S(2)}) %collective-permute-start.7) | collective-permute-done | bytes 1114144 | tf_op jit(solution)/shard_map/ppermute | solution.py:20
  242.5 4.4 collective-permute-done.6
  246.9 11.0 %pad_maximum_fusion.1 = (f32[64,20,8,136]{3,2,1,0:T(8,128)}, f32[64,20,8,136]{3,2,1,0:T(8,128)}) fusion(f32[64,4,8,136]{3,2,1,0:T(8,128)S(1)} %collective-permute-done.6, f32[64,16,8,4]{3,2,1,0:T(8,128)S(1)} %copy-done.9, f32[64,16,8,128]{3,2,1,0:T(8,128)S(1)} %copy-done, f32[64,16,8,4]{3,2,1,0:T(8,128)S(1)} %copy-done.12, ...), kind=kLoop, calls=%fused_computation.69 | loop fusion | flops 8355840 | bytes 17825792 | tf_op jit(solution)/shard_map/concatenate | solution.py:24
  257.9 12.4 %select_maximum_fusion.8 = f32[64,24,16,136]{3,2,1,0:T(8,128)} fusion(f32[64,4,8,136]{3,2,1,0:T(8,128)S(1)} %collective-permute-done.6, f32[64,4,8,136]{3,2,1,0:T(8,128)S(1)} %collective-permute-done.7, f32[64,16,8,4]{3,2,1,0:T(8,128)S(1)} %copy-done.9, f32[64,16,8,128]{3,2,1,0:T(8,128)S(1)} %copy-done, f32[64,16,8,4]{3,2,1,0:T(8,128)S(1)} %copy-done.12), kind=kLoop, calls=%fused_computation.10 | loop fusion | flops 40108032 | bytes 20054016 | tf_op jit(solution)/shard_map/concatenate | solution.py:24
  270.4 88.6 %fusion.50 = f32[64,16,8,128]{3,2,1,0:T(8,128)} fusion(f32[64,16,8,4]{3,2,1,0:T(8,128)} %copy.95, f32[64,16,8,128]{3,2,1,0:T(8,128)} %fusion.1, f32[64,16,8,4]{3,2,1,0:T(8,128)} %copy.96, f32[64,24,16,136]{3,2,1,0:T(8,128)} %select_maximum_fusion.8, f32[64,20,8,136]{3,2,1,0:T(8,128)} %get-tuple-element.30, f32[64,20,8,136]{3,2,1,0:T(8,128)} %get-tuple-element.29, ...), kind=kLoop, calls=%fused_computation.125 | loop fusion | flops 42991616 | bytes 80019456 | tf_op jit(solution)/shard_map/add | solution.py:72
  359.0 8.2 fusion.135
  367.1 3.7 copy.100
  372.1 3.7 copy.99
  375.8 4.9 collective-permute-start.8
  380.8 4.6 copy.102
  385.4 4.5 copy.101
  389.8 4.7 pad_maximum_fusion.15
  394.5 2.9 collective-permute-start.11
  399.3 21.0 %collective-permute-done.11 = f32[64,4,8,136]{3,2,1,0:T(8,128)S(1)} collective-permute-done((f32[64,4,8,136]{3,2,1,0:T(8,128)S(1)}, f32[64,4,8,136]{3,2,1,0:T(8,128)S(1)}, u32[]{:S(2)}, u32[]{:S(2)}) %collective-permute-start.11) | collective-permute-done | bytes 1114144 | tf_op jit(solution)/shard_map/ppermute | solution.py:20
  420.4 4.4 collective-permute-done.10
  424.8 11.0 %pad_maximum_fusion.2 = (f32[64,20,8,136]{3,2,1,0:T(8,128)}, f32[64,20,8,136]{3,2,1,0:T(8,128)}) fusion(f32[64,4,8,136]{3,2,1,0:T(8,128)S(1)} %collective-permute-done.10, f32[64,16,8,4]{3,2,1,0:T(8,128)S(1)} %copy-done.10, f32[64,16,8,128]{3,2,1,0:T(8,128)S(1)} %copy-done.2, f32[64,16,8,4]{3,2,1,0:T(8,128)S(1)} %copy-done.13, ...), kind=kLoop, calls=%fused_computation.71 | loop fusion | flops 8355840 | bytes 17825792 | tf_op jit(solution)/shard_map/concatenate | solution.py:24
  435.8 12.4 %select_maximum_fusion.4 = f32[64,24,16,136]{3,2,1,0:T(8,128)} fusion(f32[64,4,8,136]{3,2,1,0:T(8,128)S(1)} %collective-permute-done.10, f32[64,4,8,136]{3,2,1,0:T(8,128)S(1)} %collective-permute-done.11, f32[64,16,8,4]{3,2,1,0:T(8,128)S(1)} %copy-done.10, f32[64,16,8,128]{3,2,1,0:T(8,128)S(1)} %copy-done.2, f32[64,16,8,4]{3,2,1,0:T(8,128)S(1)} %copy-done.13), kind=kLoop, calls=%fused_computation.6 | loop fusion | flops 40108032 | bytes 20054016 | tf_op jit(solution)/shard_map/concatenate | solution.py:24
  448.2 89.1 %fusion.29 = f32[64,16,8,128]{3,2,1,0:T(8,128)} fusion(f32[64,16,8,4]{3,2,1,0:T(8,128)} %copy.101, f32[64,16,8,128]{3,2,1,0:T(8,128)} %fusion.50, f32[64,16,8,4]{3,2,1,0:T(8,128)} %copy.102, f32[64,24,16,136]{3,2,1,0:T(8,128)} %select_maximum_fusion.4, f32[64,20,8,136]{3,2,1,0:T(8,128)} %get-tuple-element.26, f32[64,20,8,136]{3,2,1,0:T(8,128)} %get-tuple-element.25, ...), kind=kLoop, calls=%fused_computation.104 | loop fusion | flops 42991616 | bytes 80019456 | tf_op jit(solution)/shard_map/add | solution.py:72
  537.3 8.2 fusion.134
  545.4 3.7 copy.106
  549.1 3.7 copy.105
  552.8 4.1 collective-permute-start.12
  559.0 5.5 collective-permute-done.13
  564.5 4.6 copy.108
  569.0 4.6 copy.107
  573.6 4.7 pad_maximum_fusion.12
  578.3 3.7 collective-permute-start.15
  584.0 4.7 fusion.113
  588.7 4.7 fusion.116
  593.4 4.8 fusion.119
  598.2 6.8 collective-permute-done.15
  605.0 4.7 collective-permute-done.14
  609.7 11.0 %pad_maximum_fusion.3 = (f32[64,20,8,136]{3,2,1,0:T(8,128)}, f32[64,20,8,136]{3,2,1,0:T(8,128)}) fusion(f32[64,4,8,136]{3,2,1,0:T(8,128)S(1)} %collective-permute-done.14, f32[64,16,8,4]{3,2,1,0:T(8,128)S(1)} %copy-done.6, f32[64,16,8,128]{3,2,1,0:T(8,128)S(1)} %copy-done.4, f32[64,16,8,4]{3,2,1,0:T(8,128)S(1)} %copy-done.7, ...), kind=kLoop, calls=%fused_computation.73 | loop fusion | flops 8355840 | bytes 17825792 | tf_op jit(solution)/shard_map/concatenate | solution.py:24
  620.7 12.4 %select_maximum_fusion = f32[64,24,16,136]{3,2,1,0:T(8,128)} fusion(f32[64,4,8,136]{3,2,1,0:T(8,128)S(1)} %collective-permute-done.14, f32[64,4,8,136]{3,2,1,0:T(8,128)S(1)} %collective-permute-done.15, f32[64,16,8,4]{3,2,1,0:T(8,128)S(1)} %copy-done.6, f32[64,16,8,128]{3,2,1,0:T(8,128)S(1)} %copy-done.4, f32[64,16,8,4]{3,2,1,0:T(8,128)S(1)} %copy-done.7), kind=kLoop, calls=%fused_computation.2 | loop fusion | flops 40108032 | bytes 20054016 | tf_op jit(solution)/shard_map/concatenate | solution.py:24
  633.2 89.8 %fusion.8 = f32[64,16,8,128]{3,2,1,0:T(8,128)} fusion(f32[64,16,8,4]{3,2,1,0:T(8,128)} %copy.107, f32[64,16,8,128]{3,2,1,0:T(8,128)} %fusion.29, f32[64,16,8,4]{3,2,1,0:T(8,128)} %copy.108, f32[64,24,16,136]{3,2,1,0:T(8,128)} %select_maximum_fusion, f32[64,20,8,136]{3,2,1,0:T(8,128)} %get-tuple-element.22, f32[64,20,8,136]{3,2,1,0:T(8,128)} %get-tuple-element.21, ...), kind=kLoop, calls=%fused_computation.83 | loop fusion | flops 42991616 | bytes 80019456 | tf_op jit(solution)/shard_map/add | solution.py:72
  723.0 6.7 fusion.122
  730.0 70.9 %psum.7 = f32[64,64]{0,1:T(8,128)S(1)} all-reduce(f32[64,64]{0,1:T(8,128)S(1)} %convolution_bitcast_fusion), channel_id=1, replica_groups=mesh['grp'=4,'slab'=32] {'grp','slab'}, use_global_device_ids=true, to_apply=%region_2.3 | all-reduce | flops 4096 | bytes 32768 | tf_op jit(solution)/shard_map/psum | solution.py:109
  801.0 5.8 cholesky.16
  807.9 5.5 all-to-all-start
  815.4 4.9 custom-call.7
  820.3 2.1 all-to-all-done
  (67 shorter events, 15.5 us)
Async XLA Ops:
  12.5 10.4 %collective-permute-start.1 = (f32[64,16,8,4]{0,2,3,1:T(8,128)S(1)}, f32[64,16,8,4]{0,2,3,1:T(8,128)S(1)}, u32[]{:S(2)}, u32[]{:S(2)}) collective-permute-start(f32[64,16,8,4]{0,2,3,1:T(8,128)S(1)} %copy.123), channel_id=1, source_target_pairs={{32,0},{64,32},{96,64},{33,1},{65,33},{97,65},{34,2},{66,34},{98,6... | collective-permute-start | bytes 393224 | tf_op jit(solution)/shard_map/ppermute | solution.py:23
  17.5 10.0 %collective-permute-start = (f32[64,16,8,4]{0,2,3,1:T(8,128)S(1)}, f32[64,16,8,4]{0,2,3,1:T(8,128)S(1)}, u32[]{:S(2)}, u32[]{:S(2)}) collective-permute-start(f32[64,16,8,4]{0,2,3,1:T(8,128)S(1)} %copy.122), channel_id=1, source_target_pairs={{0,32},{32,64},{64,96},{1,33},{33,65},{65,97},{2,34},{34,66},{66,9... | collective-permute-start | bytes 393224 | tf_op jit(solution)/shard_map/ppermute | solution.py:20
  32.0 36.9 %copy-start.5 = (f32[64,16,8,128]{3,2,1,0:T(8,128)S(1)}, f32[64,16,8,128]{3,2,1,0:T(8,128)}, u32[]{:S(2)}) copy-start(f32[64,16,8,128]{3,2,1,0:T(8,128)} %param.5) | copy-start | bytes 12582916
  32.0 36.9 %copy-start.8 = (f32[64,16,8,4]{3,2,1,0:T(8,128)S(1)}, f32[64,16,8,4]{3,2,1,0:T(8,128)}, u32[]{:S(2)}) copy-start(f32[64,16,8,4]{3,2,1,0:T(8,128)} %copy.90) | copy-start | bytes 393220
  32.0 36.9 %copy-start.11 = (f32[64,16,8,4]{3,2,1,0:T(8,128)S(1)}, f32[64,16,8,4]{3,2,1,0:T(8,128)}, u32[]{:S(2)}) copy-start(f32[64,16,8,4]{3,2,1,0:T(8,128)} %copy.89) | copy-start | bytes 393220
  36.7 27.8 %collective-permute-start.3 = (f32[64,4,8,136]{3,2,1,0:T(8,128)S(1)}, f32[64,4,8,136]{3,2,1,0:T(8,128)S(1)}, u32[]{:S(2)}, u32[]{:S(2)}) collective-permute-start(f32[64,4,8,136]{3,2,1,0:T(8,128)S(1)} %get-tuple-element.35), channel_id=1, source_target_pairs={{0,1},{1,2},{2,3},{3,4},{4,5},{5,6},{6,7},{7,8},{8,9},{9,10},{10,1... | collective-permute-start | bytes 3342344 | tf_op jit(solution)/shard_map/ppermute | solution.py:20
  41.5 27.4 %collective-permute-start.2 = (f32[64,4,8,136]{3,2,1,0:T(8,128)S(1)}, f32[64,4,8,136]{3,2,1,0:T(8,128)S(1)}, u32[]{:S(2)}, u32[]{:S(2)}) collective-permute-start(f32[64,4,8,136]{3,2,1,0:T(8,128)S(1)} %get-tuple-element.36), channel_id=1, source_target_pairs={{1,0},{2,1},{3,2},{4,3},{5,4},{6,5},{7,6},{8,7},{9,8},{10,9},{11,1... | collective-permute-start | bytes 3342344 | tf_op jit(solution)/shard_map/ppermute | solution.py:23
  79.9 12.4 %copy-start.14 = (f32[16,8,128]{2,1,0:T(8,128)S(1)}, f32[16,8,128]{2,1,0:T(8,128)}, u32[]{:S(2)}) copy-start(f32[16,8,128]{2,1,0:T(8,128)} %param.6) | copy-start | bytes 196612
  192.6 9.8 %collective-permute-start.5 = (f32[64,16,8,4]{0,2,3,1:T(8,128)S(1)}, f32[64,16,8,4]{0,2,3,1:T(8,128)S(1)}, u32[]{:S(2)}, u32[]{:S(2)}) collective-permute-start(f32[64,16,8,4]{0,2,3,1:T(8,128)S(1)} %copy.94), channel_id=1, source_target_pairs={{32,0},{64,32},{96,64},{33,1},{65,33},{97,65},{34,2},{66,34},{98,6... | collective-permute-start | bytes 393224 | tf_op jit(solution)/shard_map/ppermute | solution.py:23
  197.6 9.4 %collective-permute-start.4 = (f32[64,16,8,4]{0,2,3,1:T(8,128)S(1)}, f32[64,16,8,4]{0,2,3,1:T(8,128)S(1)}, u32[]{:S(2)}, u32[]{:S(2)}) collective-permute-start(f32[64,16,8,4]{0,2,3,1:T(8,128)S(1)} %copy.93), channel_id=1, source_target_pairs={{0,32},{32,64},{64,96},{1,33},{33,65},{65,97},{2,34},{34,66},{66,9... | collective-permute-start | bytes 393224 | tf_op jit(solution)/shard_map/ppermute | solution.py:20
  211.5 35.5 %copy-start = (f32[64,16,8,128]{3,2,1,0:T(8,128)S(1)}, f32[64,16,8,128]{3,2,1,0:T(8,128)}, u32[]{:S(2)}) copy-start(f32[64,16,8,128]{3,2,1,0:T(8,128)} %fusion.1) | copy-start | bytes 12582916
  211.5 35.5 %copy-start.9 = (f32[64,16,8,4]{3,2,1,0:T(8,128)S(1)}, f32[64,16,8,4]{3,2,1,0:T(8,128)}, u32[]{:S(2)}) copy-start(f32[64,16,8,4]{3,2,1,0:T(8,128)} %copy.96) | copy-start | bytes 393220
  211.5 35.5 %copy-start.12 = (f32[64,16,8,4]{3,2,1,0:T(8,128)S(1)}, f32[64,16,8,4]{3,2,1,0:T(8,128)}, u32[]{:S(2)}) copy-start(f32[64,16,8,4]{3,2,1,0:T(8,128)} %copy.95) | copy-start | bytes 393220
  216.1 26.4 %collective-permute-start.7 = (f32[64,4,8,136]{3,2,1,0:T(8,128)S(1)}, f32[64,4,8,136]{3,2,1,0:T(8,128)S(1)}, u32[]{:S(2)}, u32[]{:S(2)}) collective-permute-start(f32[64,4,8,136]{3,2,1,0:T(8,128)S(1)} %get-tuple-element.31), channel_id=1, source_target_pairs={{0,1},{1,2},{2,3},{3,4},{4,5},{5,6},{6,7},{7,8},{8,9},{9,10},{10,1... | collective-permute-start | bytes 3342344 | tf_op jit(solution)/shard_map/ppermute | solution.py:20
  219.6 27.4 %collective-permute-start.6 = (f32[64,4,8,136]{3,2,1,0:T(8,128)S(1)}, f32[64,4,8,136]{3,2,1,0:T(8,128)S(1)}, u32[]{:S(2)}, u32[]{:S(2)}) collective-permute-start(f32[64,4,8,136]{3,2,1,0:T(8,128)S(1)} %get-tuple-element.32), channel_id=1, source_target_pairs={{1,0},{2,1},{3,2},{4,3},{5,4},{6,5},{7,6},{8,7},{9,8},{10,9},{11,1... | collective-permute-start | bytes 3342344 | tf_op jit(solution)/shard_map/ppermute | solution.py:23
  370.8 9.9 %collective-permute-start.9 = (f32[64,16,8,4]{0,2,3,1:T(8,128)S(1)}, f32[64,16,8,4]{0,2,3,1:T(8,128)S(1)}, u32[]{:S(2)}, u32[]{:S(2)}) collective-permute-start(f32[64,16,8,4]{0,2,3,1:T(8,128)S(1)} %copy.100), channel_id=1, source_target_pairs={{32,0},{64,32},{96,64},{33,1},{65,33},{97,65},{34,2},{66,34},{98,6... | collective-permute-start | bytes 393224 | tf_op jit(solution)/shard_map/ppermute | solution.py:23
  375.8 9.5 %collective-permute-start.8 = (f32[64,16,8,4]{0,2,3,1:T(8,128)S(1)}, f32[64,16,8,4]{0,2,3,1:T(8,128)S(1)}, u32[]{:S(2)}, u32[]{:S(2)}) collective-permute-start(f32[64,16,8,4]{0,2,3,1:T(8,128)S(1)} %copy.99), channel_id=1, source_target_pairs={{0,32},{32,64},{64,96},{1,33},{33,65},{65,97},{2,34},{34,66},{66,9... | collective-permute-start | bytes 393224 | tf_op jit(solution)/shard_map/ppermute | solution.py:20
  389.8 34.9 %copy-start.2 = (f32[64,16,8,128]{3,2,1,0:T(8,128)S(1)}, f32[64,16,8,128]{3,2,1,0:T(8,128)}, u32[]{:S(2)}) copy-start(f32[64,16,8,128]{3,2,1,0:T(8,128)} %fusion.50) | copy-start | bytes 12582916
  389.8 34.9 %copy-start.10 = (f32[64,16,8,4]{3,2,1,0:T(8,128)S(1)}, f32[64,16,8,4]{3,2,1,0:T(8,128)}, u32[]{:S(2)}) copy-start(f32[64,16,8,4]{3,2,1,0:T(8,128)} %copy.102) | copy-start | bytes 393220
  389.8 34.9 %copy-start.13 = (f32[64,16,8,4]{3,2,1,0:T(8,128)S(1)}, f32[64,16,8,4]{3,2,1,0:T(8,128)}, u32[]{:S(2)}) copy-start(f32[64,16,8,4]{3,2,1,0:T(8,128)} %copy.101) | copy-start | bytes 393220
  394.5 25.9 %collective-permute-start.11 = (f32[64,4,8,136]{3,2,1,0:T(8,128)S(1)}, f32[64,4,8,136]{3,2,1,0:T(8,128)S(1)}, u32[]{:S(2)}, u32[]{:S(2)}) collective-permute-start(f32[64,4,8,136]{3,2,1,0:T(8,128)S(1)} %get-tuple-element.27), channel_id=1, source_target_pairs={{0,1},{1,2},{2,3},{3,4},{4,5},{5,6},{6,7},{7,8},{8,9},{9,10},{10,1... | collective-permute-start | bytes 3342344 | tf_op jit(solution)/shard_map/ppermute | solution.py:20
  397.4 27.4 %collective-permute-start.10 = (f32[64,4,8,136]{3,2,1,0:T(8,128)S(1)}, f32[64,4,8,136]{3,2,1,0:T(8,128)S(1)}, u32[]{:S(2)}, u32[]{:S(2)}) collective-permute-start(f32[64,4,8,136]{3,2,1,0:T(8,128)S(1)} %get-tuple-element.28), channel_id=1, source_target_pairs={{1,0},{2,1},{3,2},{4,3},{5,4},{6,5},{7,6},{8,7},{9,8},{10,9},{11,1... | collective-permute-start | bytes 3342344 | tf_op jit(solution)/shard_map/ppermute | solution.py:23
  545.4 13.2 %copy-start.16 = (s32[64,1]{0,1:T(1,128)S(1)}, s32[64,1]{0,1:T(1,128)}, u32[]{:S(2)}) copy-start(s32[64,1]{0,1:T(1,128)} %param.8) | copy-start | bytes 772
  552.8 16.2 %collective-permute-start.12 = (f32[64,16,8,4]{0,2,3,1:T(8,128)S(1)}, f32[64,16,8,4]{0,2,3,1:T(8,128)S(1)}, u32[]{:S(2)}, u32[]{:S(2)}) collective-permute-start(f32[64,16,8,4]{0,2,3,1:T(8,128)S(1)} %copy.105), channel_id=1, source_target_pairs={{0,32},{32,64},{64,96},{1,33},{33,65},{65,97},{2,34},{34,66},{66,9... | collective-permute-start | bytes 393224 | tf_op jit(solution)/shard_map/ppermute | solution.py:20
  557.0 7.5 collective-permute-start.13
  573.6 10.4 %copy-start.1 = (f32[64,16,8,128]{3,2,1,0:T(8,128)S(1)}, f32[64,16,8,128]{3,2,1,0:T(8,128)}, u32[]{:S(2)}) copy-start(f32[64,16,8,128]{3,2,1,0:T(8,128)} %fusion.1) | copy-start | bytes 12582916
  573.6 10.4 %copy-start.15 = (s32[64]{0:T(128)S(1)}, s32[64]{0:T(128)}, u32[]{:S(2)}) copy-start(s32[64]{0:T(128)} %param.7) | copy-start | bytes 772
  573.6 36.1 %copy-start.7 = (f32[64,16,8,4]{3,2,1,0:T(8,128)S(1)}, f32[64,16,8,4]{3,2,1,0:T(8,128)}, u32[]{:S(2)}) copy-start(f32[64,16,8,4]{3,2,1,0:T(8,128)} %copy.107) | copy-start | bytes 393220
  578.3 10.4 %copy-start.3 = (f32[64,16,8,128]{3,2,1,0:T(8,128)S(1)}, f32[64,16,8,128]{3,2,1,0:T(8,128)}, u32[]{:S(2)}) copy-start(f32[64,16,8,128]{3,2,1,0:T(8,128)} %fusion.50) | copy-start | bytes 12582916
  578.3 26.7 %collective-permute-start.15 = (f32[64,4,8,136]{3,2,1,0:T(8,128)S(1)}, f32[64,4,8,136]{3,2,1,0:T(8,128)S(1)}, u32[]{:S(2)}, u32[]{:S(2)}) collective-permute-start(f32[64,4,8,136]{3,2,1,0:T(8,128)S(1)} %get-tuple-element.23), channel_id=1, source_target_pairs={{0,1},{1,2},{2,3},{3,4},{4,5},{5,6},{6,7},{7,8},{8,9},{9,10},{10,1... | collective-permute-start | bytes 3342344 | tf_op jit(solution)/shard_map/ppermute | solution.py:20
  582.0 27.7 %collective-permute-start.14 = (f32[64,4,8,136]{3,2,1,0:T(8,128)S(1)}, f32[64,4,8,136]{3,2,1,0:T(8,128)S(1)}, u32[]{:S(2)}, u32[]{:S(2)}) collective-permute-start(f32[64,4,8,136]{3,2,1,0:T(8,128)S(1)} %get-tuple-element.24), channel_id=1, source_target_pairs={{1,0},{2,1},{3,2},{4,3},{5,4},{6,5},{7,6},{8,7},{9,8},{10,9},{11,1... | collective-permute-start | bytes 3342344 | tf_op jit(solution)/shard_map/ppermute | solution.py:23
  584.0 9.4 %copy-start.4 = (f32[64,16,8,128]{3,2,1,0:T(8,128)S(1)}, f32[64,16,8,128]{3,2,1,0:T(8,128)}, u32[]{:S(2)}) copy-start(f32[64,16,8,128]{3,2,1,0:T(8,128)} %fusion.29) | copy-start | bytes 12582916
  588.7 21.0 %copy-start.6 = (f32[64,16,8,4]{3,2,1,0:T(8,128)S(1)}, f32[64,16,8,4]{3,2,1,0:T(8,128)}, u32[]{:S(2)}) copy-start(f32[64,16,8,4]{3,2,1,0:T(8,128)} %copy.108) | copy-start | bytes 393220
  723.0 6.7 copy-start.17
  807.9 14.5 %all-to-all-start = ((f32[32,8,256]{2,1,0:T(8,128)}), f32[32,8,256]{2,1,0:T(8,128)S(1)}, u32[]{:S(2)}, u32[]{:S(2)}) async-start(f32[32,8,256]{2,1,0:T(8,128)} %fusion.126), calls=%async_computation | async-start | bytes 524288 | tf_op jit(solution)/shard_map/all_to_all | solution.py:101
where the time goes:
time: 832 us; the launch traced here: 825 us
  other arithmetic  481 us (58%)
  local copies, waits for them, and re-layouts  101 us (12%)
  waiting for transfers between devices  95.1 us (11%)
  blocking collectives  70.9 us (9%)
  starting transfers between devices  52.9 us (6%)
  matrix products  22.8 us (3%)
    add x4, other arithmetic, per_device(): advanced = 2.0 * current - previous + speed * laplace(pad_middle(extended))  356 us
    concatenate x12, other arithmetic, with_halo(): block = jnp.concatenate([low, block, high], axis=dim)  112 us
    psum x1, blocking collectives, per_device(): lower = jnp.linalg.cholesky(lax.psum(gram, ('grp', 'slab')))  70.9 us
    ppermute x8, waiting for transfers between devices, with_halo(): lax.ppermute(lax.slice_in_dim(block, block.shape[dim] - width, None, axis...  69.3 us
    slice x7, local copies, waits for them, and re-layouts, with_halo(): lax.slice_in_dim(block, 0, width, axis=dim)  43.7 us
    ppermute x8, starting transfers between devices, with_halo(): lax.ppermute(lax.slice_in_dim(block, block.shape[dim] - width, None, axis...  33.6 us
    ppermute x8, waiting for transfers between devices, with_halo(): lax.ppermute(lax.slice_in_dim(block, 0, width, axis=dim), axis, backward)  23.7 us
    dot_general x4, matrix products, per_device(): jnp.dot(current.reshape(PROBES, cells), picker, preferred_element_type=jn...  20.8 us
  transfers between devices with their start and end apart: 17, of which 11 were waited for; matrix products, arithmetic and copies ran while one was open for 6% of the time, Pallas kernels for 0%

commit v1 on v0

--- a/solution.py
+++ b/solution.py
@@ -1,3 +1,4 @@
+import functools
 import math
 import jax
 import jax.numpy as jnp
@@ -10,6 +11,15 @@
 CZ = 128
 STEPS = 4
 stencil_weights = (-205.0 / 72.0, 8.0 / 5.0, -1.0 / 5.0, 8.0 / 315.0, -1.0 / 560.0)
+
+
+def carry_the_things(sample, chip_axis, mesh_ax):
+    for num in (chip_axis, mesh_ax):
+        sample = jax.lax.psum(sample, num)
+    return sample
+
+
+point_pairs_all = functools.partial(carry_the_things, chip_axis="grp", mesh_ax="slab")
 
 
 def with_halo(block, sides, width):
@@ -106,7 +116,7 @@
         tiled=True,
     )
     incoming = incoming.reshape(n_slab * capacity, STEPS * PROBES)
-    lower = jnp.linalg.cholesky(lax.psum(gram, ("grp", "slab")))
+    lower = jnp.linalg.cholesky(point_pairs_all(gram))
     row_count = rec_count * n_slab * n_group * STEPS
     r_factor = lower.T / math.sqrt(row_count)
     solved = jax.scipy.linalg.solve_triangular(

time: 832 us -> 902 us (1.084)
  blocking collectives: 70.9 us -> 132 us
    psum x1 -> x2, blocking collectives: 70.9 us -> 132 us  [carry_the_things(): sample = jax.lax.psum(sample, num)]
where the time goes in v1:
time: 902 us; the launch traced here: 895 us
  other arithmetic  486 us (54%)
  blocking collectives  132 us (15%)
  local copies, waits for them, and re-layouts  100 us (11%)
  waiting for transfers between devices  95.1 us (11%)
  starting transfers between devices  57.1 us (6%)
  matrix products  22.8 us (3%)
    add x4, other arithmetic, per_device(): advanced = 2.0 * current - previous + speed * laplace(pad_middle(extended))  361 us
    psum x2, blocking collectives, carry_the_things(): sample = jax.lax.psum(sample, num)  132 us
    concatenate x12, other arithmetic, with_halo(): block = jnp.concatenate([low, block, high], axis=dim)  112 us
    ppermute x8, waiting for transfers between devices, with_halo(): lax.ppermute(lax.slice_in_dim(block, block.shape[dim] - width, None, axis...  69.3 us
    slice x7, local copies, waits for them, and re-layouts, with_halo(): lax.slice_in_dim(block, 0, width, axis=dim)  43.8 us
    ppermute x8, starting transfers between devices, with_halo(): lax.ppermute(lax.slice_in_dim(block, block.shape[dim] - width, None, axis...  34.1 us
    ppermute x8, waiting for transfers between devices, with_halo(): lax.ppermute(lax.slice_in_dim(block, 0, width, axis=dim), axis, backward)  23.6 us
    dot_general x4, matrix products, per_device(): jnp.dot(current.reshape(PROBES, cells), picker, preferred_element_type=jn...  20.8 us
  transfers between devices with their start and end apart: 17, of which 11 were waited for; matrix products, arithmetic and copies ran while one was open for 6% of the time, Pallas kernels for 0%

profile of v1, /device:TPU:1, one launch (start us, length us, event | category | flops | bytes accessed | tf_op | source)
XLA Modules:
  0.0 895.1 jit_solution(15041402818365297041)
XLA Ops:
  0.6 8.2 fusion.137
  8.8 3.7 copy.123
  13.8 3.7 copy.122
  17.5 5.0 collective-permute-start
  22.9 4.6 copy.90
  27.4 4.5 copy.89
  31.9 4.7 pad_maximum_fusion.21
  36.6 4.9 collective-permute-start.3
  43.6 20.9 %collective-permute-done.3 = f32[64,4,8,136]{3,2,1,0:T(8,128)S(1)} collective-permute-done((f32[64,4,8,136]{3,2,1,0:T(8,128)S(1)}, f32[64,4,8,136]{3,2,1,0:T(8,128)S(1)}, u32[]{:S(2)}, u32[]{:S(2)}) %collective-permute-start.3) | collective-permute-done | bytes 1114144 | tf_op jit(solution)/shard_map/ppermute | solution.py:30
  64.5 4.4 collective-permute-done.2
  68.9 11.0 %pad_maximum_fusion = (f32[64,20,8,136]{3,2,1,0:T(8,128)}, f32[64,20,8,136]{3,2,1,0:T(8,128)}) fusion(f32[64,4,8,136]{3,2,1,0:T(8,128)S(1)} %collective-permute-done.2, f32[64,16,8,4]{3,2,1,0:T(8,128)S(1)} %copy-done.8, f32[64,16,8,128]{3,2,1,0:T(8,128)S(1)} %copy-done.5, f32[64,16,8,4]{3,2,1,0:T(8,128)S(1)} %copy-done.11, ...), kind=kLoop, calls=%fused_computation.67 | loop fusion | flops 8355840 | bytes 17825792 | tf_op jit(solution)/shard_map/concatenate | solution.py:34
  79.9 12.4 %select_maximum_fusion.12 = f32[64,24,16,136]{3,2,1,0:T(8,128)} fusion(f32[64,4,8,136]{3,2,1,0:T(8,128)S(1)} %collective-permute-done.2, f32[64,4,8,136]{3,2,1,0:T(8,128)S(1)} %collective-permute-done.3, f32[64,16,8,4]{3,2,1,0:T(8,128)S(1)} %copy-done.8, f32[64,16,8,128]{3,2,1,0:T(8,128)S(1)} %copy-done.5, f32[64,16,8,4]{3,2,1,0:T(8,128)S(1)} %copy-done.11), kind=kLoop, calls=%fused_computation.14 | loop fusion | flops 40108032 | bytes 20054016 | tf_op jit(solution)/shard_map/concatenate | solution.py:34
  92.3 88.5 %fusion.1 = f32[64,16,8,128]{3,2,1,0:T(8,128)} fusion(f32[64,16,8,128]{3,2,1,0:T(8,128)} %param.5, f32[64,16,8,4]{3,2,1,0:T(8,128)} %copy.89, f32[64,16,8,4]{3,2,1,0:T(8,128)} %copy.90, f32[64,24,16,136]{3,2,1,0:T(8,128)} %select_maximum_fusion.12, f32[64,20,8,136]{3,2,1,0:T(8,128)} %get-tuple-element.34, f32[64,20,8,136]{3,2,1,0:T(8,128)} %get-tuple-element.33, ...), kind=kLoop, calls=%fused_computation.76 | loop fusion | flops 42991616 | bytes 75825152 | tf_op jit(solution)/shard_map/add | solution.py:82
  180.8 8.2 fusion.136
  188.9 3.7 copy.94
  193.9 3.7 copy.93
  197.6 4.7 collective-permute-start.4
  202.4 4.5 copy.96
  206.9 4.5 copy.95
  211.4 4.7 pad_maximum_fusion.18
  216.1 3.5 collective-permute-start.7
  219.6 2.3 collective-permute-start.6
  221.9 20.6 %collective-permute-done.7 = f32[64,4,8,136]{3,2,1,0:T(8,128)S(1)} collective-permute-done((f32[64,4,8,136]{3,2,1,0:T(8,128)S(1)}, f32[64,4,8,136]{3,2,1,0:T(8,128)S(1)}, u32[]{:S(2)}, u32[]{:S(2)}) %collective-permute-start.7) | collective-permute-done | bytes 1114144 | tf_op jit(solution)/shard_map/ppermute | solution.py:30
  242.6 4.4 collective-permute-done.6
  247.0 11.0 %pad_maximum_fusion.1 = (f32[64,20,8,136]{3,2,1,0:T(8,128)}, f32[64,20,8,136]{3,2,1,0:T(8,128)}) fusion(f32[64,4,8,136]{3,2,1,0:T(8,128)S(1)} %collective-permute-done.6, f32[64,16,8,4]{3,2,1,0:T(8,128)S(1)} %copy-done.9, f32[64,16,8,128]{3,2,1,0:T(8,128)S(1)} %copy-done, f32[64,16,8,4]{3,2,1,0:T(8,128)S(1)} %copy-done.12, ...), kind=kLoop, calls=%fused_computation.69 | loop fusion | flops 8355840 | bytes 17825792 | tf_op jit(solution)/shard_map/concatenate | solution.py:34
  258.0 12.4 %select_maximum_fusion.8 = f32[64,24,16,136]{3,2,1,0:T(8,128)} fusion(f32[64,4,8,136]{3,2,1,0:T(8,128)S(1)} %collective-permute-done.6, f32[64,4,8,136]{3,2,1,0:T(8,128)S(1)} %collective-permute-done.7, f32[64,16,8,4]{3,2,1,0:T(8,128)S(1)} %copy-done.9, f32[64,16,8,128]{3,2,1,0:T(8,128)S(1)} %copy-done, f32[64,16,8,4]{3,2,1,0:T(8,128)S(1)} %copy-done.12), kind=kLoop, calls=%fused_computation.10 | loop fusion | flops 40108032 | bytes 20054016 | tf_op jit(solution)/shard_map/concatenate | solution.py:34
  270.4 90.5 %fusion.50 = f32[64,16,8,128]{3,2,1,0:T(8,128)} fusion(f32[64,16,8,4]{3,2,1,0:T(8,128)} %copy.95, f32[64,16,8,128]{3,2,1,0:T(8,128)} %fusion.1, f32[64,16,8,4]{3,2,1,0:T(8,128)} %copy.96, f32[64,24,16,136]{3,2,1,0:T(8,128)} %select_maximum_fusion.8, f32[64,20,8,136]{3,2,1,0:T(8,128)} %get-tuple-element.30, f32[64,20,8,136]{3,2,1,0:T(8,128)} %get-tuple-element.29, ...), kind=kLoop, calls=%fused_computation.125 | loop fusion | flops 42991616 | bytes 80019456 | tf_op jit(solution)/shard_map/add | solution.py:82
  360.9 8.2 fusion.135
  369.2 3.7 copy.100
  374.1 3.7 copy.99
  377.9 4.9 collective-permute-start.8
  382.8 4.5 copy.102
  387.3 4.5 copy.101
  391.8 4.7 pad_maximum_fusion.15
  396.4 3.0 collective-permute-start.11
  401.4 21.0 %collective-permute-done.11 = f32[64,4,8,136]{3,2,1,0:T(8,128)S(1)} collective-permute-done((f32[64,4,8,136]{3,2,1,0:T(8,128)S(1)}, f32[64,4,8,136]{3,2,1,0:T(8,128)S(1)}, u32[]{:S(2)}, u32[]{:S(2)}) %collective-permute-start.11) | collective-permute-done | bytes 1114144 | tf_op jit(solution)/shard_map/ppermute | solution.py:30
  422.4 4.4 collective-permute-done.10
  426.8 11.0 %pad_maximum_fusion.2 = (f32[64,20,8,136]{3,2,1,0:T(8,128)}, f32[64,20,8,136]{3,2,1,0:T(8,128)}) fusion(f32[64,4,8,136]{3,2,1,0:T(8,128)S(1)} %collective-permute-done.10, f32[64,16,8,4]{3,2,1,0:T(8,128)S(1)} %copy-done.10, f32[64,16,8,128]{3,2,1,0:T(8,128)S(1)} %copy-done.2, f32[64,16,8,4]{3,2,1,0:T(8,128)S(1)} %copy-done.13, ...), kind=kLoop, calls=%fused_computation.71 | loop fusion | flops 8355840 | bytes 17825792 | tf_op jit(solution)/shard_map/concatenate | solution.py:34
  437.8 12.4 %select_maximum_fusion.4 = f32[64,24,16,136]{3,2,1,0:T(8,128)} fusion(f32[64,4,8,136]{3,2,1,0:T(8,128)S(1)} %collective-permute-done.10, f32[64,4,8,136]{3,2,1,0:T(8,128)S(1)} %collective-permute-done.11, f32[64,16,8,4]{3,2,1,0:T(8,128)S(1)} %copy-done.10, f32[64,16,8,128]{3,2,1,0:T(8,128)S(1)} %copy-done.2, f32[64,16,8,4]{3,2,1,0:T(8,128)S(1)} %copy-done.13), kind=kLoop, calls=%fused_computation.6 | loop fusion | flops 40108032 | bytes 20054016 | tf_op jit(solution)/shard_map/concatenate | solution.py:34
  450.3 90.3 %fusion.29 = f32[64,16,8,128]{3,2,1,0:T(8,128)} fusion(f32[64,16,8,4]{3,2,1,0:T(8,128)} %copy.101, f32[64,16,8,128]{3,2,1,0:T(8,128)} %fusion.50, f32[64,16,8,4]{3,2,1,0:T(8,128)} %copy.102, f32[64,24,16,136]{3,2,1,0:T(8,128)} %select_maximum_fusion.4, f32[64,20,8,136]{3,2,1,0:T(8,128)} %get-tuple-element.26, f32[64,20,8,136]{3,2,1,0:T(8,128)} %get-tuple-element.25, ...), kind=kLoop, calls=%fused_computation.104 | loop fusion | flops 42991616 | bytes 80019456 | tf_op jit(solution)/shard_map/add | solution.py:82
  540.6 8.2 fusion.134
  548.7 3.7 copy.106
  552.4 3.7 copy.105
  556.1 4.1 collective-permute-start.12
  562.3 5.5 collective-permute-done.13
  567.8 4.5 copy.108
  572.3 4.5 copy.107
  576.8 4.7 pad_maximum_fusion.12
  581.4 3.8 collective-permute-start.15
  587.3 4.7 fusion.113
  591.9 4.7 fusion.116
  596.6 4.8 fusion.119
  601.4 6.8 collective-permute-done.15
  608.2 4.6 collective-permute-done.14
  612.9 11.0 %pad_maximum_fusion.3 = (f32[64,20,8,136]{3,2,1,0:T(8,128)}, f32[64,20,8,136]{3,2,1,0:T(8,128)}) fusion(f32[64,4,8,136]{3,2,1,0:T(8,128)S(1)} %collective-permute-done.14, f32[64,16,8,4]{3,2,1,0:T(8,128)S(1)} %copy-done.6, f32[64,16,8,128]{3,2,1,0:T(8,128)S(1)} %copy-done.4, f32[64,16,8,4]{3,2,1,0:T(8,128)S(1)} %copy-done.7, ...), kind=kLoop, calls=%fused_computation.73 | loop fusion | flops 8355840 | bytes 17825792 | tf_op jit(solution)/shard_map/concatenate | solution.py:34
  623.9 12.4 %select_maximum_fusion = f32[64,24,16,136]{3,2,1,0:T(8,128)} fusion(f32[64,4,8,136]{3,2,1,0:T(8,128)S(1)} %collective-permute-done.14, f32[64,4,8,136]{3,2,1,0:T(8,128)S(1)} %collective-permute-done.15, f32[64,16,8,4]{3,2,1,0:T(8,128)S(1)} %copy-done.6, f32[64,16,8,128]{3,2,1,0:T(8,128)S(1)} %copy-done.4, f32[64,16,8,4]{3,2,1,0:T(8,128)S(1)} %copy-done.7), kind=kLoop, calls=%fused_computation.2 | loop fusion | flops 40108032 | bytes 20054016 | tf_op jit(solution)/shard_map/concatenate | solution.py:34
  636.3 92.0 %fusion.8 = f32[64,16,8,128]{3,2,1,0:T(8,128)} fusion(f32[64,16,8,4]{3,2,1,0:T(8,128)} %copy.107, f32[64,16,8,128]{3,2,1,0:T(8,128)} %fusion.29, f32[64,16,8,4]{3,2,1,0:T(8,128)} %copy.108, f32[64,24,16,136]{3,2,1,0:T(8,128)} %select_maximum_fusion, f32[64,20,8,136]{3,2,1,0:T(8,128)} %get-tuple-element.22, f32[64,20,8,136]{3,2,1,0:T(8,128)} %get-tuple-element.21, ...), kind=kLoop, calls=%fused_computation.83 | loop fusion | flops 42991616 | bytes 80019456 | tf_op jit(solution)/shard_map/add | solution.py:82
  728.3 6.7 fusion.122
  735.3 13.8 %psum.14 = f32[64,64]{0,1:T(8,128)S(1)} all-reduce(f32[64,64]{0,1:T(8,128)S(1)} %convolution_bitcast_fusion), channel_id=1, replica_groups=mesh['grp'=4,'slab'=32] {'grp'}, use_global_device_ids=true, to_apply=%region_2.3 | all-reduce | flops 4096 | bytes 32768 | tf_op jit(solution)/shard_map/psum | solution.py:18
  749.1 118.6 %psum.15 = f32[64,64]{0,1:T(8,128)S(1)} all-reduce(f32[64,64]{0,1:T(8,128)S(1)} %psum.14), channel_id=1, replica_groups=mesh['grp'=4,'slab'=32] {'slab'}, use_global_device_ids=true, to_apply=%region_3.4 | all-reduce | flops 4096 | bytes 32768 | tf_op jit(solution)/shard_map/psum | solution.py:18
  867.8 5.8 cholesky.16
  874.7 9.2 %all-to-all-start = ((f32[32,8,256]{2,1,0:T(8,128)}), f32[32,8,256]{2,1,0:T(8,128)S(1)}, u32[]{:S(2)}, u32[]{:S(2)}) async-start(f32[32,8,256]{2,1,0:T(8,128)} %fusion.126), calls=%async_computation | async-start | bytes 524288 | tf_op jit(solution)/shard_map/all_to_all | solution.py:111
  885.8 4.9 custom-call.7
  890.7 2.2 all-to-all-done
  (68 shorter events, 17.6 us)
Async XLA Ops:
  12.5 10.4 %collective-permute-start.1 = (f32[64,16,8,4]{0,2,3,1:T(8,128)S(1)}, f32[64,16,8,4]{0,2,3,1:T(8,128)S(1)}, u32[]{:S(2)}, u32[]{:S(2)}) collective-permute-start(f32[64,16,8,4]{0,2,3,1:T(8,128)S(1)} %copy.123), channel_id=1, source_target_pairs={{32,0},{64,32},{96,64},{33,1},{65,33},{97,65},{34,2},{66,34},{98,6... | collective-permute-start | bytes 393224 | tf_op jit(solution)/shard_map/ppermute | solution.py:33
  17.5 9.9 %collective-permute-start = (f32[64,16,8,4]{0,2,3,1:T(8,128)S(1)}, f32[64,16,8,4]{0,2,3,1:T(8,128)S(1)}, u32[]{:S(2)}, u32[]{:S(2)}) collective-permute-start(f32[64,16,8,4]{0,2,3,1:T(8,128)S(1)} %copy.122), channel_id=1, source_target_pairs={{0,32},{32,64},{64,96},{1,33},{33,65},{65,97},{2,34},{34,66},{66,9... | collective-permute-start | bytes 393224 | tf_op jit(solution)/shard_map/ppermute | solution.py:30
  31.9 37.0 %copy-start.5 = (f32[64,16,8,128]{3,2,1,0:T(8,128)S(1)}, f32[64,16,8,128]{3,2,1,0:T(8,128)}, u32[]{:S(2)}) copy-start(f32[64,16,8,128]{3,2,1,0:T(8,128)} %param.5) | copy-start | bytes 12582916
  31.9 37.0 %copy-start.8 = (f32[64,16,8,4]{3,2,1,0:T(8,128)S(1)}, f32[64,16,8,4]{3,2,1,0:T(8,128)}, u32[]{:S(2)}) copy-start(f32[64,16,8,4]{3,2,1,0:T(8,128)} %copy.90) | copy-start | bytes 393220
  31.9 37.0 %copy-start.11 = (f32[64,16,8,4]{3,2,1,0:T(8,128)S(1)}, f32[64,16,8,4]{3,2,1,0:T(8,128)}, u32[]{:S(2)}) copy-start(f32[64,16,8,4]{3,2,1,0:T(8,128)} %copy.89) | copy-start | bytes 393220
  36.6 27.9 %collective-permute-start.3 = (f32[64,4,8,136]{3,2,1,0:T(8,128)S(1)}, f32[64,4,8,136]{3,2,1,0:T(8,128)S(1)}, u32[]{:S(2)}, u32[]{:S(2)}) collective-permute-start(f32[64,4,8,136]{3,2,1,0:T(8,128)S(1)} %get-tuple-element.35), channel_id=1, source_target_pairs={{0,1},{1,2},{2,3},{3,4},{4,5},{5,6},{6,7},{7,8},{8,9},{9,10},{10,1... | collective-permute-start | bytes 3342344 | tf_op jit(solution)/shard_map/ppermute | solution.py:30
  41.5 27.4 %collective-permute-start.2 = (f32[64,4,8,136]{3,2,1,0:T(8,128)S(1)}, f32[64,4,8,136]{3,2,1,0:T(8,128)S(1)}, u32[]{:S(2)}, u32[]{:S(2)}) collective-permute-start(f32[64,4,8,136]{3,2,1,0:T(8,128)S(1)} %get-tuple-element.36), channel_id=1, source_target_pairs={{1,0},{2,1},{3,2},{4,3},{5,4},{6,5},{7,6},{8,7},{9,8},{10,9},{11,1... | collective-permute-start | bytes 3342344 | tf_op jit(solution)/shard_map/ppermute | solution.py:33
  79.9 12.4 %copy-start.14 = (f32[16,8,128]{2,1,0:T(8,128)S(1)}, f32[16,8,128]{2,1,0:T(8,128)}, u32[]{:S(2)}) copy-start(f32[16,8,128]{2,1,0:T(8,128)} %param.6) | copy-start | bytes 196612
  192.6 9.8 %collective-permute-start.5 = (f32[64,16,8,4]{0,2,3,1:T(8,128)S(1)}, f32[64,16,8,4]{0,2,3,1:T(8,128)S(1)}, u32[]{:S(2)}, u32[]{:S(2)}) collective-permute-start(f32[64,16,8,4]{0,2,3,1:T(8,128)S(1)} %copy.94), channel_id=1, source_target_pairs={{32,0},{64,32},{96,64},{33,1},{65,33},{97,65},{34,2},{66,34},{98,6... | collective-permute-start | bytes 393224 | tf_op jit(solution)/shard_map/ppermute | solution.py:33
  197.6 9.3 %collective-permute-start.4 = (f32[64,16,8,4]{0,2,3,1:T(8,128)S(1)}, f32[64,16,8,4]{0,2,3,1:T(8,128)S(1)}, u32[]{:S(2)}, u32[]{:S(2)}) collective-permute-start(f32[64,16,8,4]{0,2,3,1:T(8,128)S(1)} %copy.93), channel_id=1, source_target_pairs={{0,32},{32,64},{64,96},{1,33},{33,65},{65,97},{2,34},{34,66},{66,9... | collective-permute-start | bytes 393224 | tf_op jit(solution)/shard_map/ppermute | solution.py:30
  211.4 35.6 %copy-start = (f32[64,16,8,128]{3,2,1,0:T(8,128)S(1)}, f32[64,16,8,128]{3,2,1,0:T(8,128)}, u32[]{:S(2)}) copy-start(f32[64,16,8,128]{3,2,1,0:T(8,128)} %fusion.1) | copy-start | bytes 12582916
  211.4 35.6 %copy-start.9 = (f32[64,16,8,4]{3,2,1,0:T(8,128)S(1)}, f32[64,16,8,4]{3,2,1,0:T(8,128)}, u32[]{:S(2)}) copy-start(f32[64,16,8,4]{3,2,1,0:T(8,128)} %copy.96) | copy-start | bytes 393220
  211.4 35.6 %copy-start.12 = (f32[64,16,8,4]{3,2,1,0:T(8,128)S(1)}, f32[64,16,8,4]{3,2,1,0:T(8,128)}, u32[]{:S(2)}) copy-start(f32[64,16,8,4]{3,2,1,0:T(8,128)} %copy.95) | copy-start | bytes 393220
  216.1 26.5 %collective-permute-start.7 = (f32[64,4,8,136]{3,2,1,0:T(8,128)S(1)}, f32[64,4,8,136]{3,2,1,0:T(8,128)S(1)}, u32[]{:S(2)}, u32[]{:S(2)}) collective-permute-start(f32[64,4,8,136]{3,2,1,0:T(8,128)S(1)} %get-tuple-element.31), channel_id=1, source_target_pairs={{0,1},{1,2},{2,3},{3,4},{4,5},{5,6},{6,7},{7,8},{8,9},{9,10},{10,1... | collective-permute-start | bytes 3342344 | tf_op jit(solution)/shard_map/ppermute | solution.py:30
  219.6 27.4 %collective-permute-start.6 = (f32[64,4,8,136]{3,2,1,0:T(8,128)S(1)}, f32[64,4,8,136]{3,2,1,0:T(8,128)S(1)}, u32[]{:S(2)}, u32[]{:S(2)}) collective-permute-start(f32[64,4,8,136]{3,2,1,0:T(8,128)S(1)} %get-tuple-element.32), channel_id=1, source_target_pairs={{1,0},{2,1},{3,2},{4,3},{5,4},{6,5},{7,6},{8,7},{9,8},{10,9},{11,1... | collective-permute-start | bytes 3342344 | tf_op jit(solution)/shard_map/ppermute | solution.py:33
  372.9 9.9 %collective-permute-start.9 = (f32[64,16,8,4]{0,2,3,1:T(8,128)S(1)}, f32[64,16,8,4]{0,2,3,1:T(8,128)S(1)}, u32[]{:S(2)}, u32[]{:S(2)}) collective-permute-start(f32[64,16,8,4]{0,2,3,1:T(8,128)S(1)} %copy.100), channel_id=1, source_target_pairs={{32,0},{64,32},{96,64},{33,1},{65,33},{97,65},{34,2},{66,34},{98,6... | collective-permute-start | bytes 393224 | tf_op jit(solution)/shard_map/ppermute | solution.py:33
  377.9 9.4 %collective-permute-start.8 = (f32[64,16,8,4]{0,2,3,1:T(8,128)S(1)}, f32[64,16,8,4]{0,2,3,1:T(8,128)S(1)}, u32[]{:S(2)}, u32[]{:S(2)}) collective-permute-start(f32[64,16,8,4]{0,2,3,1:T(8,128)S(1)} %copy.99), channel_id=1, source_target_pairs={{0,32},{32,64},{64,96},{1,33},{33,65},{65,97},{2,34},{34,66},{66,9... | collective-permute-start | bytes 393224 | tf_op jit(solution)/shard_map/ppermute | solution.py:30
  391.8 35.0 %copy-start.2 = (f32[64,16,8,128]{3,2,1,0:T(8,128)S(1)}, f32[64,16,8,128]{3,2,1,0:T(8,128)}, u32[]{:S(2)}) copy-start(f32[64,16,8,128]{3,2,1,0:T(8,128)} %fusion.50) | copy-start | bytes 12582916
  391.8 35.0 %copy-start.10 = (f32[64,16,8,4]{3,2,1,0:T(8,128)S(1)}, f32[64,16,8,4]{3,2,1,0:T(8,128)}, u32[]{:S(2)}) copy-start(f32[64,16,8,4]{3,2,1,0:T(8,128)} %copy.102) | copy-start | bytes 393220
  391.8 35.0 %copy-start.13 = (f32[64,16,8,4]{3,2,1,0:T(8,128)S(1)}, f32[64,16,8,4]{3,2,1,0:T(8,128)}, u32[]{:S(2)}) copy-start(f32[64,16,8,4]{3,2,1,0:T(8,128)} %copy.101) | copy-start | bytes 393220
  396.4 26.0 %collective-permute-start.11 = (f32[64,4,8,136]{3,2,1,0:T(8,128)S(1)}, f32[64,4,8,136]{3,2,1,0:T(8,128)S(1)}, u32[]{:S(2)}, u32[]{:S(2)}) collective-permute-start(f32[64,4,8,136]{3,2,1,0:T(8,128)S(1)} %get-tuple-element.27), channel_id=1, source_target_pairs={{0,1},{1,2},{2,3},{3,4},{4,5},{5,6},{6,7},{7,8},{8,9},{9,10},{10,1... | collective-permute-start | bytes 3342344 | tf_op jit(solution)/shard_map/ppermute | solution.py:30
  399.4 27.4 %collective-permute-start.10 = (f32[64,4,8,136]{3,2,1,0:T(8,128)S(1)}, f32[64,4,8,136]{3,2,1,0:T(8,128)S(1)}, u32[]{:S(2)}, u32[]{:S(2)}) collective-permute-start(f32[64,4,8,136]{3,2,1,0:T(8,128)S(1)} %get-tuple-element.28), channel_id=1, source_target_pairs={{1,0},{2,1},{3,2},{4,3},{5,4},{6,5},{7,6},{8,7},{9,8},{10,9},{11,1... | collective-permute-start | bytes 3342344 | tf_op jit(solution)/shard_map/ppermute | solution.py:33
  548.7 13.2 %copy-start.16 = (s32[64,1]{0,1:T(1,128)S(1)}, s32[64,1]{0,1:T(1,128)}, u32[]{:S(2)}) copy-start(s32[64,1]{0,1:T(1,128)} %param.8) | copy-start | bytes 772
  556.1 16.1 %collective-permute-start.12 = (f32[64,16,8,4]{0,2,3,1:T(8,128)S(1)}, f32[64,16,8,4]{0,2,3,1:T(8,128)S(1)}, u32[]{:S(2)}, u32[]{:S(2)}) collective-permute-start(f32[64,16,8,4]{0,2,3,1:T(8,128)S(1)} %copy.105), channel_id=1, source_target_pairs={{0,32},{32,64},{64,96},{1,33},{33,65},{65,97},{2,34},{34,66},{66,9... | collective-permute-start | bytes 393224 | tf_op jit(solution)/shard_map/ppermute | solution.py:30
  560.3 7.5 collective-permute-start.13
  576.7 10.5 %copy-start.1 = (f32[64,16,8,128]{3,2,1,0:T(8,128)S(1)}, f32[64,16,8,128]{3,2,1,0:T(8,128)}, u32[]{:S(2)}) copy-start(f32[64,16,8,128]{3,2,1,0:T(8,128)} %fusion.1) | copy-start | bytes 12582916
  576.7 10.5 %copy-start.15 = (s32[64]{0:T(128)S(1)}, s32[64]{0:T(128)}, u32[]{:S(2)}) copy-start(s32[64]{0:T(128)} %param.7) | copy-start | bytes 772
  576.7 36.1 %copy-start.7 = (f32[64,16,8,4]{3,2,1,0:T(8,128)S(1)}, f32[64,16,8,4]{3,2,1,0:T(8,128)}, u32[]{:S(2)}) copy-start(f32[64,16,8,4]{3,2,1,0:T(8,128)} %copy.107) | copy-start | bytes 393220
  581.4 10.5 %copy-start.3 = (f32[64,16,8,128]{3,2,1,0:T(8,128)S(1)}, f32[64,16,8,128]{3,2,1,0:T(8,128)}, u32[]{:S(2)}) copy-start(f32[64,16,8,128]{3,2,1,0:T(8,128)} %fusion.50) | copy-start | bytes 12582916
  581.4 26.8 %collective-permute-start.15 = (f32[64,4,8,136]{3,2,1,0:T(8,128)S(1)}, f32[64,4,8,136]{3,2,1,0:T(8,128)S(1)}, u32[]{:S(2)}, u32[]{:S(2)}) collective-permute-start(f32[64,4,8,136]{3,2,1,0:T(8,128)S(1)} %get-tuple-element.23), channel_id=1, source_target_pairs={{0,1},{1,2},{2,3},{3,4},{4,5},{5,6},{6,7},{7,8},{8,9},{9,10},{10,1... | collective-permute-start | bytes 3342344 | tf_op jit(solution)/shard_map/ppermute | solution.py:30
  585.3 27.6 %collective-permute-start.14 = (f32[64,4,8,136]{3,2,1,0:T(8,128)S(1)}, f32[64,4,8,136]{3,2,1,0:T(8,128)S(1)}, u32[]{:S(2)}, u32[]{:S(2)}) collective-permute-start(f32[64,4,8,136]{3,2,1,0:T(8,128)S(1)} %get-tuple-element.24), channel_id=1, source_target_pairs={{1,0},{2,1},{3,2},{4,3},{5,4},{6,5},{7,6},{8,7},{9,8},{10,9},{11,1... | collective-permute-start | bytes 3342344 | tf_op jit(solution)/shard_map/ppermute | solution.py:33
  587.3 9.3 %copy-start.4 = (f32[64,16,8,128]{3,2,1,0:T(8,128)S(1)}, f32[64,16,8,128]{3,2,1,0:T(8,128)}, u32[]{:S(2)}) copy-start(f32[64,16,8,128]{3,2,1,0:T(8,128)} %fusion.29) | copy-start | bytes 12582916
  591.9 20.9 %copy-start.6 = (f32[64,16,8,4]{3,2,1,0:T(8,128)S(1)}, f32[64,16,8,4]{3,2,1,0:T(8,128)}, u32[]{:S(2)}) copy-start(f32[64,16,8,4]{3,2,1,0:T(8,128)} %copy.108) | copy-start | bytes 393220
  728.3 6.7 copy-start.17
  874.7 18.3 %all-to-all-start = ((f32[32,8,256]{2,1,0:T(8,128)}), f32[32,8,256]{2,1,0:T(8,128)S(1)}, u32[]{:S(2)}, u32[]{:S(2)}) async-start(f32[32,8,256]{2,1,0:T(8,128)} %fusion.126), calls=%async_computation | async-start | bytes 524288 | tf_op jit(solution)/shard_map/all_to_all | solution.py:111
